TPU v7x, 32 devices: a whole 2x2x4 slice. The times are simulated.
32 devices in a mesh: ctx: 8 (over y, x, core), fsdp: 4 (over z).
Axes of the slice: x: 2, y: 2, z: 4, core: 2. Of those that a mesh axis runs over, the one named last changes fastest.
Arguments:
- layer_in: bfloat16 [8, 1024, 1024], P('fsdp', 'ctx'), may hold values from -6 to 6
- block_order: int32 [8, 16], P('fsdp'), may hold values from 0 to 15, as said below
- ln1_gain: bfloat16 [1024], P('fsdp'), may hold values from 0.5 to 1.5
- ln1_shift: bfloat16 [1024], P('fsdp'), may hold values from -3 to 3
- w_qkv: bfloat16 [1024, 3072], P('fsdp'), may hold values from -0.1875 to 0.1875
- b_query: bfloat16 [1024], P('fsdp'), may hold values from -3 to 3
- b_value: bfloat16 [1024], P('fsdp'), may hold values from -3 to 3
- w_out: bfloat16 [1024, 1024], P('fsdp'), may hold values from -1 to 1
- b_out: bfloat16 [1024], P('fsdp'), may hold values from -2 to 2
- ln2_gain: bfloat16 [1024], P('fsdp'), may hold values from 0.5 to 1.5
- ln2_shift: bfloat16 [1024], P('fsdp'), may hold values from -3 to 3
- w_up: bfloat16 [1024, 4096], P('fsdp'), may hold values from -0.1875 to 0.1875
- b_up: bfloat16 [4096], P('fsdp'), may hold values from -3 to 3
- w_down: bfloat16 [4096, 1024], P('fsdp'), may hold values from -0.09375 to 0.09375
- b_down: bfloat16 [1024], P('fsdp'), may hold values from -3 to 3
- cotangent: bfloat16 [8, 1024, 1024], P('fsdp', 'ctx'), may hold values from -6 to 6
Outputs:
- layer_out: bfloat16 [8, 1024, 1024], P('fsdp', 'ctx')
- input_grad: bfloat16 [8, 1024, 1024], P('fsdp', 'ctx')
- grad_ln1_gain: float32 [1024], P(('ctx', 'fsdp'))
- grad_ln1_shift: float32 [1024], P(('ctx', 'fsdp'))
- grad_w_qkv: float32 [1024, 3072], P(('ctx', 'fsdp'))
- grad_b_query: float32 [1024], P(('ctx', 'fsdp'))
- grad_b_value: float32 [1024], P(('ctx', 'fsdp'))
- grad_w_out: float32 [1024, 1024], P(('ctx', 'fsdp'))
- grad_b_out: float32 [1024], P(('ctx', 'fsdp'))
- grad_ln2_gain: float32 [1024], P(('ctx', 'fsdp'))
- grad_ln2_shift: float32 [1024], P(('ctx', 'fsdp'))
- grad_w_up: float32 [1024, 4096], P(('ctx', 'fsdp'))
- grad_b_up: float32 [4096], P(('ctx', 'fsdp'))
- grad_w_down: float32 [4096, 1024], P(('ctx', 'fsdp'))
- grad_b_down: float32 [1024], P(('ctx', 'fsdp'))
Inputs may be any that keep to these rules, and one draw needn't show every extreme that they name: Stored block j of sequence s (rows j * 64 to (j + 1) * 64 - 1 as stored) holds block block_order[s, j] of the true order; each row is a permutation, and entry 2c + 1 is 15 minus entry 2c.
All inputs are finite; a program needn't handle non-finite values.
Results may differ from a plain program's by a relative error of at most 0.012.
Values may be sent and summed in bfloat16 or wider, within the bound.
A program may use at most 512 MiB of HBM per device.

v0:
```python
import math
import types

import jax
import jax.numpy as jnp
from jax import lax
from jax.experimental import pallas as pl
from jax.experimental.pallas import tpu as pltpu
from jax.sharding import PartitionSpec as P

D = 1024
HEADS = 8
HEAD_DIM = 128


EPSILON = 1e-05
NEG_LARGE = -1e30
GELU_C = math.sqrt(2.0 / math.pi)
GELU_K = 0.044715
VMEM_BYTES = 63 << 20


def gelu_tanh(values):
    inner = jnp.tanh(GELU_C * (values + GELU_K * values * values * values))
    return 0.5 * values * (1.0 + inner)


def gelu_slope(values):
    inner = jnp.tanh(GELU_C * (values + GELU_K * values * values * values))
    return 0.5 * (1.0 + inner) + 0.5 * values * (1.0 - inner * inner) * GELU_C * (
        1.0 + 3.0 * GELU_K * values * values
    )


def normalize(values, gain_vec, shift_vec):
    average = jnp.mean(values, axis=-1, keepdims=True)
    centered = values - average
    inv_dev = lax.rsqrt(jnp.mean(centered * centered, axis=-1, keepdims=True) + EPSILON)
    normed = centered * inv_dev
    return (normed * gain_vec + shift_vec, normed, inv_dev)


def normalize_back(grad, normed, inv_dev, gain_vec):
    scaled = grad * gain_vec
    return inv_dev * (
        scaled
        - jnp.mean(scaled, axis=-1, keepdims=True)
        - normed * jnp.mean(scaled * normed, axis=-1, keepdims=True)
    )


def token_positions(order_row, seq_len, half_rows):
    rows = jnp.arange(seq_len, dtype=jnp.int32)
    slots = jnp.arange(order_row.shape[0], dtype=jnp.int32)
    picked = jnp.sum(
        jnp.where((rows // half_rows)[:, None] == slots[None, :], order_row[None, :], 0), axis=1
    )
    return picked * half_rows + rows % half_rows


def block_probs(query_heads, key_heads, query_pos, key_pos, row_lse, scale):
    raw_scores = jnp.einsum(
        "qhd,khd->hqk", query_heads, key_heads, preferred_element_type=jnp.float32
    )
    allowed = (query_pos[:, None] >= key_pos[None, :])[None]
    shifted = jnp.where(allowed, raw_scores * scale - row_lse[:, :, None], NEG_LARGE)
    return jnp.where(allowed, jnp.exp(shifted), 0.0)


def score_grads(probs, grad_probs, row_delta, scale):
    return (probs * (grad_probs - row_delta[:, :, None]) * scale).astype(jnp.bfloat16)


def per_device_ctx(
    layer_in,
    block_order,
    ln1_gain,
    ln1_shift,
    w_qkv,
    b_query,
    b_value,
    w_out,
    b_out,
    ln2_gain,
    ln2_shift,
    w_up,
    b_up,
    w_down,
    b_down,
    cotangent,
):
    full = (
        lax.all_gather(ln1_gain, "fsdp", axis=0, tiled=True),
        lax.all_gather(ln1_shift, "fsdp", axis=0, tiled=True),
        lax.all_gather(w_qkv, "fsdp", axis=0, tiled=True),
        lax.all_gather(b_query, "fsdp", axis=0, tiled=True),
        lax.all_gather(b_value, "fsdp", axis=0, tiled=True),
        lax.all_gather(w_out, "fsdp", axis=0, tiled=True),
        lax.all_gather(b_out, "fsdp", axis=0, tiled=True),
        lax.all_gather(ln2_gain, "fsdp", axis=0, tiled=True),
        lax.all_gather(ln2_shift, "fsdp", axis=0, tiled=True),
        lax.all_gather(w_up, "fsdp", axis=0, tiled=True),
        lax.all_gather(b_up, "fsdp", axis=0, tiled=True),
        lax.all_gather(w_down, "fsdp", axis=0, tiled=True),
        lax.all_gather(b_down, "fsdp", axis=0, tiled=True),
    )
    qkv_full, out_full, up_full, down_full = (full[2], full[5], full[9], full[11])
    first_gain = full[0].astype(jnp.float32)
    first_shift = full[1].astype(jnp.float32)
    query_bias = full[3].astype(jnp.float32)
    value_bias = full[4].astype(jnp.float32)
    out_bias = full[6].astype(jnp.float32)
    second_gain = full[7].astype(jnp.float32)
    second_shift = full[8].astype(jnp.float32)
    up_bias = full[10].astype(jnp.float32)
    down_bias = full[12].astype(jnp.float32)
    micro = layer_in.shape[0]
    tokens = layer_in.shape[1]
    seq_len = tokens * lax.axis_size("ctx")
    half_rows = tokens // 2
    key_block = min(512, seq_len)
    blocks = seq_len // key_block
    scale = HEAD_DIM ** (-0.5)
    here = lax.axis_index("ctx")
    heads_shape = (blocks, key_block, HEADS, HEAD_DIM)
    totals = [jnp.zeros(item.shape, jnp.float32) for item in full]
    outputs_fwd = []
    outputs_grad = []
    for micro_step in range(micro):
        pos_all = token_positions(block_order[micro_step], seq_len, half_rows)
        pos_mine = lax.dynamic_slice_in_dim(pos_all, here * tokens, tokens)
        pos_blocks = pos_all.reshape(blocks, key_block)
        inputs = layer_in[micro_step].astype(jnp.float32)
        first_out, first_normed, first_inv = normalize(inputs, first_gain, first_shift)
        first_low = first_out.astype(jnp.bfloat16)
        projected = jnp.dot(first_low, qkv_full, preferred_element_type=jnp.float32)
        query_low = (projected[:, :D] + query_bias).astype(jnp.bfloat16)
        key_low = projected[:, D : 2 * D].astype(jnp.bfloat16)
        value_low = (projected[:, 2 * D :] + value_bias).astype(jnp.bfloat16)
        keys_all, values_all = (
            lax.all_gather(key_low, "ctx", axis=0, tiled=True),
            lax.all_gather(value_low, "ctx", axis=0, tiled=True),
        )
        query_heads = query_low.reshape(tokens, HEADS, HEAD_DIM)
        key_blocks = keys_all.reshape(heads_shape)
        value_blocks = values_all.reshape(heads_shape)

        def stats_step(carry, piece):
            run_max, run_sum = carry
            key_piece, key_pos = piece
            raw_scores = (
                jnp.einsum(
                    "qhd,khd->hqk", query_heads, key_piece, preferred_element_type=jnp.float32
                )
                * scale
            )
            allowed = (pos_mine[:, None] >= key_pos[None, :])[None]
            masked = jnp.where(allowed, raw_scores, NEG_LARGE)
            new_max = jnp.maximum(run_max, jnp.max(masked, axis=-1))
            weights = jnp.where(allowed, jnp.exp(masked - new_max[:, :, None]), 0.0)
            run_sum = run_sum * jnp.exp(run_max - new_max) + jnp.sum(weights, axis=-1)
            return ((new_max, run_sum), None)

        start_state = (
            jnp.full((HEADS, tokens), NEG_LARGE, jnp.float32),
            jnp.zeros((HEADS, tokens), jnp.float32),
        )
        (run_max, run_sum), unused = lax.scan(stats_step, start_state, (key_blocks, pos_blocks))
        row_lse = run_max + jnp.log(run_sum)

        def output_step(carry, piece):
            acc_low, acc_exact = carry
            key_piece, value_piece, key_pos = piece
            probs = block_probs(query_heads, key_piece, pos_mine, key_pos, row_lse, scale)
            acc_low = acc_low + jnp.einsum(
                "hqk,khd->hqd",
                probs.astype(jnp.bfloat16),
                value_piece,
                preferred_element_type=jnp.float32,
            )
            acc_exact = acc_exact + jnp.einsum(
                "hqk,khd->hqd",
                probs,
                value_piece.astype(jnp.float32),
                preferred_element_type=jnp.float32,
            )
            return ((acc_low, acc_exact), None)

        start_acc = (
            jnp.zeros((HEADS, tokens, HEAD_DIM), jnp.float32),
            jnp.zeros((HEADS, tokens, HEAD_DIM), jnp.float32),
        )
        (attn_heads, exact_heads), unused = lax.scan(
            output_step, start_acc, (key_blocks, value_blocks, pos_blocks)
        )
        attn_low = jnp.transpose(attn_heads, (1, 0, 2)).reshape(tokens, D).astype(jnp.bfloat16)
        resid = inputs + jnp.dot(attn_low, out_full, preferred_element_type=jnp.float32) + out_bias
        second_out, second_normed, second_inv = normalize(resid, second_gain, second_shift)
        second_low = second_out.astype(jnp.bfloat16)
        hidden = jnp.dot(second_low, up_full, preferred_element_type=jnp.float32) + up_bias
        active_low = gelu_tanh(hidden).astype(jnp.bfloat16)
        result = (
            resid + jnp.dot(active_low, down_full, preferred_element_type=jnp.float32) + down_bias
        )
        outputs_fwd.append(result.astype(jnp.bfloat16))
        grad_out = cotangent[micro_step]
        grad_outf = grad_out.astype(jnp.float32)
        term_down = jnp.einsum(
            "tf,td->fd", active_low, grad_out, preferred_element_type=jnp.float32
        )
        grad_active = jnp.einsum(
            "td,fd->tf", grad_out, down_full, preferred_element_type=jnp.float32
        )
        grad_hidden = (grad_active * gelu_slope(hidden)).astype(jnp.bfloat16)
        term_up = jnp.einsum(
            "td,tf->df", second_low, grad_hidden, preferred_element_type=jnp.float32
        )
        grad_second = jnp.einsum(
            "tf,df->td", grad_hidden, up_full, preferred_element_type=jnp.float32
        )
        grad_resid = grad_outf + normalize_back(grad_second, second_normed, second_inv, second_gain)
        grad_branch = grad_resid.astype(jnp.bfloat16)
        term_out = jnp.einsum(
            "td,te->de", attn_low, grad_branch, preferred_element_type=jnp.float32
        )
        grad_attn = jnp.einsum(
            "te,de->td", grad_branch, out_full, preferred_element_type=jnp.float32
        ).astype(jnp.bfloat16)
        grad_heads = grad_attn.reshape(tokens, HEADS, HEAD_DIM)
        row_delta = jnp.einsum("qhd,hqd->hq", grad_heads.astype(jnp.float32), exact_heads)

        def backward_step(grad_query, piece):
            key_piece, value_piece, key_pos = piece
            probs = block_probs(query_heads, key_piece, pos_mine, key_pos, row_lse, scale)
            grad_value = jnp.einsum(
                "hqk,qhd->khd",
                probs.astype(jnp.bfloat16),
                grad_heads,
                preferred_element_type=jnp.float32,
            )
            grad_probs = jnp.einsum(
                "qhd,khd->hqk", grad_heads, value_piece, preferred_element_type=jnp.float32
            )
            grad_scores = score_grads(probs, grad_probs, row_delta, scale)
            grad_query = grad_query + jnp.einsum(
                "hqk,khd->qhd", grad_scores, key_piece, preferred_element_type=jnp.float32
            )
            grad_key = jnp.einsum(
                "hqk,qhd->khd", grad_scores, query_heads, preferred_element_type=jnp.float32
            )
            rows_here = key_piece.shape[0]
            return (
                grad_query,
                jnp.concatenate(
                    [grad_key.reshape(rows_here, D), grad_value.reshape(rows_here, D)], axis=1
                ),
            )

        grad_query, key_terms = lax.scan(
            backward_step,
            jnp.zeros((tokens, HEADS, HEAD_DIM), jnp.float32),
            (key_blocks, value_blocks, pos_blocks),
        )
        key_sums = lax.psum_scatter(
            key_terms.reshape(seq_len, 2 * D), "ctx", scatter_dimension=0, tiled=True
        )
        grad_key_low = key_sums[:, :D].astype(jnp.bfloat16)
        grad_value_low = key_sums[:, D:].astype(jnp.bfloat16)
        grad_query_low = grad_query.reshape(tokens, D).astype(jnp.bfloat16)
        grad_projected = jnp.concatenate([grad_query_low, grad_key_low, grad_value_low], axis=1)
        term_qkv = jnp.einsum(
            "td,te->de", first_low, grad_projected, preferred_element_type=jnp.float32
        )
        grad_first = jnp.einsum(
            "te,de->td", grad_projected, qkv_full, preferred_element_type=jnp.float32
        )
        grad_input = grad_resid + normalize_back(grad_first, first_normed, first_inv, first_gain)
        outputs_grad.append(grad_input.astype(jnp.bfloat16))
        terms = (
            jnp.sum(grad_first * first_normed, axis=0),
            jnp.sum(grad_first, axis=0),
            term_qkv,
            jnp.sum(grad_query_low.astype(jnp.float32), axis=0),
            jnp.sum(grad_value_low.astype(jnp.float32), axis=0),
            term_out,
            jnp.sum(grad_branch.astype(jnp.float32), axis=0),
            jnp.sum(grad_second * second_normed, axis=0),
            jnp.sum(grad_second, axis=0),
            term_up,
            jnp.sum(grad_hidden.astype(jnp.float32), axis=0),
            term_down,
            jnp.sum(grad_outf, axis=0),
        )
        totals = [older + newer for older, newer in zip(totals, terms)]
    summed = (
        lax.psum_scatter(totals[0], ("ctx", "fsdp"), scatter_dimension=0, tiled=True),
        lax.psum_scatter(totals[1], ("ctx", "fsdp"), scatter_dimension=0, tiled=True),
        lax.psum_scatter(totals[2], ("ctx", "fsdp"), scatter_dimension=0, tiled=True),
        lax.psum_scatter(totals[3], ("ctx", "fsdp"), scatter_dimension=0, tiled=True),
        lax.psum_scatter(totals[4], ("ctx", "fsdp"), scatter_dimension=0, tiled=True),
        lax.psum_scatter(totals[5], ("ctx", "fsdp"), scatter_dimension=0, tiled=True),
        lax.psum_scatter(totals[6], ("ctx", "fsdp"), scatter_dimension=0, tiled=True),
        lax.psum_scatter(totals[7], ("ctx", "fsdp"), scatter_dimension=0, tiled=True),
        lax.psum_scatter(totals[8], ("ctx", "fsdp"), scatter_dimension=0, tiled=True),
        lax.psum_scatter(totals[9], ("ctx", "fsdp"), scatter_dimension=0, tiled=True),
        lax.psum_scatter(totals[10], ("ctx", "fsdp"), scatter_dimension=0, tiled=True),
        lax.psum_scatter(totals[11], ("ctx", "fsdp"), scatter_dimension=0, tiled=True),
        lax.psum_scatter(totals[12], ("ctx", "fsdp"), scatter_dimension=0, tiled=True),
    )
    return (
        jnp.stack(outputs_fwd),
        jnp.stack(outputs_grad),
        summed[0],
        summed[1],
        summed[2],
        summed[3],
        summed[4],
        summed[5],
        summed[6],
        summed[7],
        summed[8],
        summed[9],
        summed[10],
        summed[11],
        summed[12],
    )


LOG2E = 1.4426950408889634


def dot_as(left, right, left_dim, right_dim):
    return lax.dot_general(
        left, right, (((left_dim,), (right_dim,)), ((), ())), preferred_element_type=jnp.float32
    )


def dot_nn(left, right):
    return dot_as(left, right, 1, 0)


def dot_nt(left, right):
    return dot_as(left, right, 1, 1)


def dot_tn(left, right):
    return dot_as(left, right, 0, 0)


class Ring:
    def __init__(self):
        self.col = lax.axis_index("ctx")
        self.layer = lax.axis_index("fsdp")
        col = self.col
        self.sib = col + 1 - 2 * (col % 2)
        self.xnb = col + 2 - 4 * ((col // 2) % 2)
        self.ynb = col + 4 - 8 * (col // 4)
        self.diag = self.xnb + self.ynb - col
        self.xsib = self.xnb + self.sib - col
        self.ysib = self.ynb + self.sib - col
        self.dsib = self.diag + self.sib - col

    def flat(self, col):
        return (col, self.layer)

    def up(self, hop):
        return (self.layer + hop) % 4


class Wire:
    def __init__(self):
        self.all = []

    def plan(self, src, dst, send_sem, recv_sem, where):
        copy = Sent(src, dst, send_sem, recv_sem, where)
        self.all.append(copy)
        return copy

    def send(self, src, dst, send_sem, recv_sem, where):
        copy = self.plan(src, dst, send_sem, recv_sem, where)
        copy.start()
        return copy

    def drain(self):
        for copy in self.all:
            copy.wait_send()


class Sent:
    def __init__(self, src, dst, send_sem, recv_sem, where):
        self.copy = pltpu.make_async_remote_copy(
            src_ref=src,
            dst_ref=dst,
            send_sem=send_sem,
            recv_sem=recv_sem,
            device_id=where,
            device_id_type=pl.DeviceIdType.MESH,
        )
        self.left = True
        self.came = False

    def start(self):
        self.copy.start()

    def copy_in(self):
        self.copy.wait_recv()

    def copy_out(self):
        self.copy.wait_send()

    def wait_recv(self):
        self.came = True
        self.copy.wait_recv()

    def wait_send(self):
        if self.left:
            self.left = False
            self.copy.wait_send()


def move(src, dst, sem):
    copy = pltpu.make_async_copy(src, dst, sem)
    copy.start()
    return copy


class Gather:
    def __init__(self, ring, wire, block, half, ssem, rsem):
        plan = (
            (half(ring.col, 0), ring.xnb),
            (half(ring.col, 1), ring.ynb),
            (block(ring.col), ring.sib),
            (half(ring.xnb, 0), ring.ynb),
            (block(ring.xnb), ring.sib),
            (half(ring.ynb, 1), ring.xnb),
            (block(ring.ynb), ring.sib),
            (block(ring.diag), ring.sib),
            (half(ring.col, 1), ring.xnb),
            (half(ring.col, 0), ring.ynb),
        )
        self.sent = [
            wire.plan(ref, ref, ssem.at[slot], rsem.at[slot], ring.flat(col))
            for slot, (ref, col) in enumerate(plan)
        ]

    def start(self):
        for slot in (0, 1, 8, 9, 2):
            self.sent[slot].start()

    def relay(self):
        self.sent[0].wait_recv()
        self.sent[3].start()
        self.sent[1].wait_recv()
        self.sent[5].start()
        self.sent[8].wait_recv()
        self.sent[4].start()
        self.sent[9].wait_recv()
        self.sent[6].start()

    def relay_diag(self):
        self.sent[3].wait_recv()
        self.sent[5].wait_recv()
        self.sent[7].start()

    def finish(self):
        for slot in (2, 4, 6, 7):
            self.sent[slot].wait_recv()

    def drain(self):
        for copy in self.sent:
            copy.wait_send()


class Scatter:
    def __init__(self, ring, wire, part, rows, from_sib, from_diag, from_side, ssem, rsem):
        self.ring, self.part, self.rows = ring, part, rows
        self.from_sib, self.from_diag, self.from_side = from_sib, from_diag, from_side
        self.ssem, self.rsem = ssem, rsem
        self.core = ring.sib % 2
        half = rows // 2
        plan = [
            (part.at[self.at(col)], from_sib.at[slot], ring.sib)
            for slot, col in enumerate((ring.sib, ring.xsib, ring.ysib, ring.dsib))
        ]
        plan += [
            (part.at[self.at(ring.diag, 0, half)], from_diag.at[0], ring.xnb),
            (part.at[self.at(ring.diag, half, half)], from_diag.at[1], ring.ynb),
            (part.at[self.at(ring.xnb, 0, half)], from_side.at[0, 0:half], ring.xnb),
            (part.at[self.at(ring.ynb, half, half)], from_side.at[1, half:rows], ring.ynb),
            (part.at[self.at(ring.xnb, half, half)], from_side.at[0, half:rows], ring.xnb),
            (part.at[self.at(ring.ynb, 0, half)], from_side.at[1, 0:half], ring.ynb),
        ]
        self.sent = [
            wire.plan(src, dst, ssem.at[slot], rsem.at[slot], ring.flat(col))
            for slot, (src, dst, col) in enumerate(plan)
        ]

    def at(self, col, first=0, count=None):
        count = self.rows if count is None else count
        return pl.ds(pl.multiple_of(col * self.rows + first, count), count)

    def start_of(self, chip, slot):
        ring = self.ring
        col = chip * 2 + self.core
        Sent(
            self.part.at[self.at(col)],
            self.from_sib.at[slot],
            self.ssem.at[slot],
            self.rsem.at[slot],
            ring.flat(ring.sib),
        ).start()

    def start(self):
        for slot in (3, 1, 2, 0):
            self.sent[slot].start()

    def add(self, col, extra, first=0, count=None):
        where = self.at(col, first, count)
        total = self.part[where].astype(jnp.float32)
        for item in extra:
            total = total + item.astype(jnp.float32)
        self.part[where] = total.astype(jnp.bfloat16)

    def middle(self):
        self.sent[3].wait_recv()
        self.add(self.ring.diag, [self.from_sib[3]])
        self.sent[4].start()
        self.sent[5].start()

    def early(self):
        half = self.rows // 2
        self.sent[1].wait_recv()
        self.add(self.ring.xnb, [self.from_sib[1, :half]], 0, half)
        self.sent[6].start()
        self.sent[2].wait_recv()
        self.add(self.ring.ynb, [self.from_sib[2, half:]], half, half)
        self.sent[7].start()

    def last(self):
        half = self.rows // 2
        self.sent[4].wait_recv()
        self.add(self.ring.ynb, [self.from_sib[2, :half], self.from_diag[0]], 0, half)
        self.sent[9].start()
        self.sent[5].wait_recv()
        self.add(self.ring.xnb, [self.from_sib[1, half:], self.from_diag[1]], half, half)
        self.sent[8].start()

    def finish(self):
        for slot in (0, 6, 7, 8, 9):
            self.sent[slot].wait_recv()
        total = self.part[self.at(self.ring.col)].astype(jnp.float32)
        total = total + self.from_sib[0].astype(jnp.float32)
        return (
            total + self.from_side[0].astype(jnp.float32) + self.from_side[1].astype(jnp.float32)
        )

    def drain(self):
        for copy in self.sent:
            copy.wait_send()


class Halve:
    def __init__(self, ring, wire, part, near, far, ssem, rsem):
        layer = ring.layer
        self.near_plane = layer + 1 - 2 * (layer % 2)
        self.far_plane = (layer + 2) % 4
        cross = (self.near_plane + 2) % 4
        self.ring, self.part, self.near, self.far = ring, part, near, far
        plan = (
            (part(cross), near.at[0], self.near_plane),
            (part(self.near_plane), near.at[1], self.near_plane),
            (part(self.far_plane), far, self.far_plane),
        )
        self.one, self.two, self.last = (
            wire.plan(src, dst, ssem.at[slot], rsem.at[slot], (ring.col, plane))
            for slot, (src, dst, plane) in enumerate(plan)
        )

    def start(self):
        self.one.start()
        self.two.start()

    def middle(self):
        self.one.wait_recv()
        ref = self.part(self.far_plane)
        total = ref[...].astype(jnp.float32) + self.near[0].astype(jnp.float32)
        ref[...] = total.astype(jnp.bfloat16)
        self.last.start()

    def finish(self):
        self.two.wait_recv()
        total = self.part(self.ring.layer)[...].astype(jnp.float32)
        total = total + self.near[1].astype(jnp.float32)
        self.last.wait_recv()
        return total + self.far[...].astype(jnp.float32)


class Chain:
    def __init__(self, ring, block, ssem, rsem):
        layer, col = ring.layer, ring.col
        self.ways = []
        for way, step in ((0, 1), (1, -1)):
            inside = layer < 3 if step > 0 else layer > 0
            copies = []
            for k in range(3):
                item = block(ring.up(4 - k * step))
                copies.append(
                    Sent(item, item, ssem.at[way, k], rsem.at[way, k], (col, ring.up(4 + step)))
                )
            reach = [layer >= k if step > 0 else layer + k <= 3 for k in range(4)]
            self.ways.append((inside, reach, copies))

    def start(self):
        for inside, _, copies in self.ways:
            pl.when(inside)(copies[0].start)

    def pass_on(self, k):
        for inside, reach, copies in self.ways:

            @pl.when(reach[k])
            def _():
                copies[k - 1].copy_in()
                if k < 3:
                    pl.when(inside)(copies[k].start)

    def drain(self):
        for inside, reach, copies in self.ways:
            for k in range(3):

                @pl.when(jnp.logical_and(inside, reach[k]))
                def _():
                    copies[k].copy_out()


def row_norm(values):
    average = jnp.mean(values, axis=-1, keepdims=True)
    centered = values - average
    inv_dev = lax.rsqrt(jnp.mean(centered * centered, axis=-1, keepdims=True) + EPSILON)
    return centered * inv_dev, inv_dev


def layer_kernel(scale, refs):
    f32, bf16 = jnp.float32, jnp.bfloat16
    ring = Ring()
    wire = Wire()
    send = wire.send
    col, layer = ring.col, ring.layer
    seqs, tokens, width = refs.x.shape
    seq_len = tokens * 8
    head = HEAD_DIM
    rows_z = width // 4
    hid = refs.wu.shape[1] // 4
    step_c2 = scale * LOG2E
    R = refs
    mine = pl.ds(pl.multiple_of(col * tokens, tokens), tokens)
    head_cols = pl.multiple_of(col * head, head)

    barrier = pltpu.get_barrier_semaphore()
    me = col * 4 + layer
    owner_col, owner_layer = 2 * layer + col // 4, col % 4
    at_home = owner_col * 4 + owner_layer == me
    for hop in range(1, 32):
        other = (me + hop) % 32
        pl.semaphore_signal(
            barrier, 1, device_id=(other // 4, other % 4), device_id_type=pl.DeviceIdType.MESH
        )
    local = R.lsem
    load_x = move(R.x, R.xb, local.at[0])
    load_ct = [move(R.cot.at[s], R.ct.at[s, mine], local.at[1 + s]) for s in range(seqs)]
    qkv_rows = pl.ds(pl.multiple_of(layer * rows_z, rows_z), rows_z)
    load_q = []
    for g in range(3):
        src = R.w_qkv.at[:, pl.ds(pl.multiple_of(g * width + col * head, head), head)]
        load_q.append(move(src, R.wq.at[qkv_rows, g * head : (g + 1) * head], local.at[3 + g]))
    small_rows = 32
    out_src = R.w_out.at[pl.ds(pl.multiple_of(col * small_rows, small_rows), small_rows)]
    load_o = move(out_src, R.wo.at[layer, col], local.at[6])
    load_u = []
    for g in range(4):
        src = R.w_up.at[:, pl.ds(pl.multiple_of(g * width + col * hid, hid), hid)]
        load_u.append(move(src, R.wu.at[qkv_rows, g * hid : (g + 1) * hid], local.at[7 + g]))
    down_src = R.w_down.at[pl.ds(pl.multiple_of(col * hid, hid), hid)]
    down_rows = pl.ds(pl.multiple_of(layer * hid, hid), hid)
    load_d = move(down_src, R.wd.at[down_rows], local.at[11])
    load_p = []
    for row, item in enumerate(R.vectors):
        load_p.append(move(item, R.pv.at[layer, row], local.at[12 + row]))
    load_b = move(R.b_up, R.pb.at[layer], local.at[11 + 9])
    load_x.wait()
    first, second = (row_norm(R.xb[s].astype(f32))[0] for s in range(2))
    R.r1[0] = first
    R.r1[1] = second
    for s in range(seqs):
        lane = lax.broadcasted_iota(jnp.int32, (1, seq_len), 1)
        half_rows = tokens // 2
        pos = jnp.zeros((1, seq_len), jnp.int32)
        down = lax.broadcasted_iota(jnp.int32, (half_rows, 128), 0)
        for j in range(seq_len // half_rows):
            start = R.order[s, j] * half_rows
            pos = jnp.where(lane // half_rows == j, start, pos)
            R.kpos[s, j * half_rows : (j + 1) * half_rows, :] = down + start
        R.qpos[s] = pos + lane % half_rows
    for copy in load_p:
        copy.wait()
    load_b.wait()
    pl.semaphore_wait(barrier, 31)

    zs, zr = R.zs, R.zr

    def to_planes(src, dst, slot):
        return [
            send(src, dst, zs.at[slot, hop - 1], zr.at[slot, hop - 1], (col, ring.up(hop)))
            for hop in range(1, 4)
        ]

    send_par = to_planes(R.pv.at[layer], R.pv.at[layer], 0)
    send_par += to_planes(R.pb.at[layer], R.pb.at[layer], 1)

    def rows_of(ref, count):
        return lambda index: ref.at[pl.ds(pl.multiple_of(index * count, count), count)]

    chain_q, chain_u, chain_d = (
        Chain(ring, rows_of(ref, count), R.cs.at[slot], R.cr.at[slot])
        for slot, (ref, count) in enumerate(((R.wq, rows_z), (R.wu, rows_z), (R.wd, hid)))
    )
    for copy in load_q:
        copy.wait()
    chain_q.start()

    def gather_rows(ref, s, slot):

        def block(index):
            return ref.at[s, pl.ds(pl.multiple_of(index * tokens, tokens), tokens)]

        def half(index, part):
            count = tokens // 2
            first = pl.multiple_of(index * tokens + part * count, count)
            return ref.at[s, pl.ds(first, count)]

        return Gather(ring, wire, block, half, R.gs.at[slot], R.gr.at[slot])

    h1_gather = [gather_rows(R.h1, s, s) for s in range(seqs)]
    ct_gather = [gather_rows(R.ct, s, 2 + s) for s in range(seqs)]
    h2_gather = [gather_rows(R.h2, s, 4 + s) for s in range(seqs)]
    wo_gather = Gather(
        ring,
        wire,
        lambda index: R.wo.at[:, index],
        lambda index, part: R.wo.at[2 * part : 2 * part + 2, index],
        R.gs.at[6],
        R.gr.at[6],
    )

    for copy in load_ct:
        copy.wait()
    ct_gather[0].start()


    def params_row(row):
        pieces = []
        for plane in range(4):
            both = R.pv[plane, row].astype(f32)
            pieces += [both[0:1, :], both[1:2, :]]
        return jnp.concatenate(pieces, axis=1)

    for copy in send_par:
        copy.wait_recv()
    gain1, shift1 = params_row(0), params_row(1)
    R.h1[0, mine] = (R.r1[0] * gain1 + shift1).astype(bf16)
    h1_gather[0].start()
    R.h1[1, mine] = (R.r1[1] * gain1 + shift1).astype(bf16)
    h1_gather[1].start()
    for copy in load_u:
        copy.wait()
    chain_u.start()
    load_o.wait()
    send_o = to_planes(out_src, R.wo.at[layer, col], 4)

    def chosen(rows):
        total = rows[0]
        for index, item in enumerate(rows[1:]):
            total = jnp.where(col == index + 1, item, total)
        return total

    def head_row(row):
        parts = [R.pv[plane, row].astype(f32) for plane in range(4)]
        return chosen([parts[j // 2][j % 2 : j % 2 + 1, :] for j in range(8)])

    bias_q, bias_v = head_row(2), head_row(3)
    pieces = []
    for plane in range(4):
        rows = R.pb[plane].astype(f32)
        pieces.append(chosen([rows[j : j + 1, :] for j in range(8)]))
    bias_u = jnp.concatenate(pieces, axis=1)
    tile = 256


    def span(chip):
        return pl.ds(pl.multiple_of(chip * tile, tile), tile)

    chip_x, chip_y = (col // 2) % 2, col // 4

    def order(t):
        flip_x, flip_y = 1 - t[0], 1 - t[1]
        place_x = chip_x + flip_x - 2 * chip_x * flip_x
        place_y = chip_y + flip_y - 2 * chip_y * flip_y
        return place_x + 2 * place_y, flip_x + 2 * flip_y

    def tiles(body, **between):
        @pl.loop(0, 2)
        def _(high):
            @pl.loop(0, 2)
            def _(low):
                body((high, low))
                t = 2 * high + low
                for name, action in between.items():
                    pl.when(t == int(name[1:]))(action)

    def project(s):
        @pl.loop(0, 4)
        def _(t):
            r = span(t)
            both = dot_nn(R.h1[s, r, :], R.wq[...])
            R.q[s, r, :] = (both[:, :head] + bias_q).astype(bf16)
            R.k[s, r, :] = both[:, head : 2 * head].astype(bf16)
            R.v[s, r, :] = (both[:, 2 * head :] + bias_v).astype(bf16)

        R.kt[s] = R.k[s].T
        R.vt[s] = R.v[s].T

    def masked(s, r, scores, other):
        keys = jnp.concatenate([R.kpos[s]] * (tile // 128), axis=1)
        return jnp.where(R.qpos[s, :, r] >= keys, scores, other)

    def attend(s, t):
        r = span(2 * t[0] + t[1])
        raw = masked(s, r, dot_nt(R.k[s], R.q[s, r, :]), NEG_LARGE)
        top = jnp.max(raw, axis=0, keepdims=True)
        weights = jnp.exp2((raw - top) * step_c2)
        total = jnp.sum(weights, axis=0, keepdims=True)
        turned = dot_nn(R.vt[s], weights.astype(bf16)) * (1.0 / total)
        R.ol[s, r, :] = turned.T.astype(bf16)
        R.lse[s, :, r] = top * step_c2 + jnp.log2(total)

    others = (ring.dsib, ring.diag, ring.xsib, ring.xnb, ring.ysib, ring.ynb, ring.sib)

    def heads_to_rows(s):
        R.ob[s, :, pl.ds(head_cols, head)] = R.ol[s, mine, :]
        copies = []
        for slot, other in enumerate(others):
            src = R.ol.at[s, pl.ds(pl.multiple_of(other * tokens, tokens), tokens)]
            dst = R.ob.at[s, :, pl.ds(head_cols, head)]
            copies.append(
                send(src, dst, R.a_s.at[s, slot], R.a_r.at[s, slot], ring.flat(other))
            )
        return copies

    def rows_to_heads(s):
        R.dh[s, mine, :] = R.db[s, :, pl.ds(head_cols, head)]
        copies = []
        for slot, other in enumerate(others):
            src = R.db.at[s, :, pl.ds(pl.multiple_of(other * head, head), head)]
            dst = R.dh.at[s, mine]
            copies.append(
                send(src, dst, R.a_s.at[2 + s, slot], R.a_r.at[2 + s, slot], ring.flat(other))
            )
        return copies

    bias_o = params_row(4)
    gain2, shift2 = params_row(5), params_row(6)
    out_w = R.wo

    def out_project(s):
        for copy in moved_o[s]:
            copy.wait_recv()
        weight = out_w[...].reshape(width, width)
        resid = R.xb[s].astype(f32) + dot_nn(R.ob[s], weight) + bias_o
        R.r1[s] = resid
        normed, _ = row_norm(resid)
        R.h2[s, mine] = (normed * gain2 + shift2).astype(bf16)

    def many(*actions):
        def run():
            for action in actions:
                action()

        return run

    ct_gather[0].relay()
    h1_gather[0].relay()
    chain_q.pass_on(1)
    h1_gather[1].relay()
    h1_gather[0].relay_diag()
    ct_gather[0].relay_diag()
    ct_gather[1].start()
    chain_q.pass_on(2)
    load_d.wait()
    chain_d.start()
    h1_gather[0].finish()
    chain_q.pass_on(3)
    project(0)
    chain_u.pass_on(1)
    h1_gather[1].relay_diag()
    for copy in send_o:
        copy.wait_recv()
    wo_gather.start()
    tiles(lambda t: attend(0, t), t2=wo_gather.relay)
    moved_o = [heads_to_rows(0)]
    h1_gather[1].finish()
    ct_gather[1].relay()
    project(1)
    wo_gather.relay_diag()
    chain_u.pass_on(2)

    def first_rows():
        out_project(0)
        h2_gather[0].start()

    tiles(
        lambda t: attend(1, t),
        t0=lambda: chain_d.pass_on(1),
        t1=many(wo_gather.finish, first_rows),
        t2=ct_gather[1].relay_diag,
    )
    moved_o.append(heads_to_rows(1))
    h2_gather[0].relay()
    chain_u.pass_on(3)
    out_project(1)
    h2_gather[1].start()
    chain_d.pass_on(2)
    h2_gather[0].relay_diag()
    ct_gather[0].finish()
    h2_gather[0].finish()
    chain_d.pass_on(3)

    def feed(s, t):
        chip, slot = order(t)
        r = span(chip)
        hidden = dot_nn(R.h2[s, r, :], R.wu[...]) + bias_u
        square = hidden * hidden
        bend = jnp.tanh(hidden * (GELU_C + (GELU_C * GELU_K) * square))
        half = 0.5 * (1.0 + bend)
        active = (hidden * half).astype(bf16)
        slope = half + (0.5 * hidden) * (1.0 - bend * bend) * (
            GELU_C + (3.0 * GELU_C * GELU_K) * square
        )
        R.act[s, r, :] = active
        R.po[s, r, :] = dot_nn(active, R.wd[...]).astype(bf16)
        grad = dot_nt(R.ct[s, r, :], R.wd[...])
        grad = (grad * slope).astype(bf16)
        R.du[s, r, :] = grad
        R.pd[s, r, :] = dot_nt(grad, R.wu[...]).astype(bf16)
        R.us[...] += jnp.sum(grad.astype(f32), axis=0, keepdims=True)
        d2[s].start_of(chip, slot)
        out_sc[s].start_of(chip, slot)

    def scatter(part, s, recv, slot, rows=None):
        return Scatter(
            ring,
            wire,
            part,
            tokens,
            R.r_sib.at[recv],
            R.r_diag.at[recv],
            R.r_side.at[recv],
            R.ss.at[slot],
            R.sr.at[slot],
        )

    R.us[...] = jnp.zeros_like(R.us)
    d2 = [scatter(R.pd.at[s], s, s, s) for s in range(2)]
    out_sc = [scatter(R.po.at[s], s, 2 + s, 2 + s) for s in range(2)]
    tiles(
        lambda t: feed(0, t),
        t0=h2_gather[1].relay,
        t1=d2[0].middle,
        t2=h2_gather[1].relay_diag,
        t3=d2[0].early,
    )
    d2[0].last()
    h2_gather[1].finish()
    ct_gather[1].finish()
    tiles(lambda t: feed(1, t), t1=d2[1].middle, t3=d2[1].early)

    bz = R.bz
    for g in range(4):
        bz[2 + g : 3 + g, :] = R.us[:, g * hid : (g + 1) * hid]


    def grad_down():
        for j in range(2):
            cols = slice(j * 2 * hid, (j + 1) * 2 * hid)
            total = dot_tn(R.act[0, :, cols], R.ct[0])
            total = total + dot_tn(R.act[1, :, cols], R.ct[1])
            R.gd[cols, :] = total.astype(bf16)

    def grad_up():
        for j in range(2):
            cols = slice(j * 2 * hid, (j + 1) * 2 * hid)
            total = dot_tn(R.du[0, :, cols], R.h2[0])
            total = total + dot_tn(R.du[1, :, cols], R.h2[1])
            total = total.T.astype(bf16).reshape(8, 4, 32, 2 * hid)
            R.gu[:, :, :, cols] = total

    def to_planes_part(piece, dst, slot):
        return [
            send(
                piece(ring.up(hop)),
                dst.at[hop - 1],
                zs.at[slot, hop - 1],
                zr.at[slot, hop - 1],
                (col, ring.up(hop)),
            )
            for hop in range(1, 4)
        ]

    sums = {}

    def back_norm2(s):
        grad = d2[s].finish()
        normed, inv_dev = row_norm(R.r1[s])
        cot = R.ct[s, mine].astype(f32)
        scaled = grad * gain2
        resid = cot + inv_dev * (
            scaled
            - jnp.mean(scaled, axis=-1, keepdims=True)
            - normed * jnp.mean(scaled * normed, axis=-1, keepdims=True)
        )
        R.dr[s] = resid
        low = resid.astype(bf16)
        R.dz[s] = low
        lowf = low.astype(f32)
        parts = (
            jnp.sum(lowf, axis=0, keepdims=True),
            jnp.sum(grad * normed, axis=0, keepdims=True),
            jnp.sum(grad, axis=0, keepdims=True),
            jnp.sum(cot, axis=0, keepdims=True),
        )
        for row, item in enumerate(parts):
            sums[row] = sums[row] + item if row in sums else item
        R.db[s] = dot_nt(low, out_w[...].reshape(width, width)).astype(bf16)

    def attend_back(s, t):
        r = span(2 * t[0] + t[1])
        query, dout = R.q[s, r, :], R.dh[s, r, :]
        raw = dot_nt(R.k[s], query)
        probs = masked(s, r, jnp.exp2(raw * step_c2 - R.lse[s, :, r]), 0.0)
        grad = dot_nt(R.v[s], dout)
        part_v = dot_nn(probs.astype(bf16), dout)
        delta = jnp.sum(probs * grad, axis=0, keepdims=True)
        low = (probs * ((grad - delta) * scale)).astype(bf16)
        part_k = dot_nn(low, query)
        R.dp[s, r, :head] = dot_nn(R.kt[s], low).T.astype(bf16)
        R.dva[s] += part_v
        R.dka[s] += part_k

    def close_back(s):
        R.dp[s, :, head : 2 * head] = R.dka[s].astype(bf16)
        R.dp[s, :, 2 * head :] = R.dva[s].astype(bf16)

    def first_part(s, t):
        chip, slot = order(t)
        r = span(chip)
        R.pd[s, r, :] = dot_nt(R.dp[s, r, :], R.wq[...]).astype(bf16)
        d1[s].start_of(chip, slot)

    back_norm2(0)
    moved_d = [rows_to_heads(0)]
    d2[1].last()
    grad_down()
    z_down = Halve(ring, wire, rows_of(R.gd, hid), R.zd.at[0:2], R.zd.at[2], zs.at[10], zr.at[10])
    z_down.start()
    out_sc[0].middle()
    grad_up()
    z_up = Halve(
        ring, wire, lambda other: R.gu.at[:, other], R.zu.at[0:2], R.zu.at[2], zs.at[11], zr.at[11]
    )
    z_up.start()
    back_norm2(1)
    moved_d.append(rows_to_heads(1))
    out_sc[0].early()
    out_sc[0].last()

    h2_flat = R.h2.at[0]
    for gather in h2_gather:
        gather.drain()
    h2_flat[...] = (dot_tn(R.ob[0], R.dz[0]) + dot_tn(R.ob[1], R.dz[1])).astype(bf16)
    wo_sc = scatter(h2_flat, 0, 4, 6)
    wo_sc.start()
    R.dva[...] = jnp.zeros_like(R.dva)
    R.dka[...] = jnp.zeros_like(R.dka)
    for copy in moved_d[0]:
        copy.wait_recv()
    tiles(lambda t: attend_back(0, t), t1=wo_sc.middle)
    close_back(0)
    d2[0].drain()
    d1 = [scatter(R.pd.at[s], s, s, 4 + s) for s in range(2)]
    tiles(lambda t: first_part(0, t))
    z_down.middle()
    for copy in moved_d[1]:
        copy.wait_recv()
    tiles(
        lambda t: attend_back(1, t),
        t0=many(d1[0].middle, d1[0].early, out_sc[1].middle),
        t2=many(d1[0].last, z_up.middle),
        t3=many(wo_sc.early, wo_sc.last),
    )
    close_back(1)
    d2[1].drain()
    tiles(lambda t: first_part(1, t), t2=d1[1].middle)
    proj_sums = jnp.sum(R.dp[0].astype(f32), axis=0, keepdims=True) + jnp.sum(
        R.dp[1].astype(f32), axis=0, keepdims=True
    )
    bz[0:1, :] = proj_sums[:, :head]
    bz[1:2, :] = proj_sums[:, 2 * head :]
    bz[6:8, :] = jnp.zeros((2, head), f32)
    z_b = to_planes(bz, R.zb.at[layer], 13)
    for g in range(3):
        cols = slice(g * head, (g + 1) * head)
        total = dot_tn(R.dp[0, :, cols], R.h1[0]) + dot_tn(R.dp[1, :, cols], R.h1[1])
        R.gq[:, :, :, cols] = total.T.astype(bf16).reshape(8, 4, 32, head)
    z_q = Halve(
        ring, wire, lambda other: R.gq.at[:, other], R.zq.at[0:2], R.zq.at[2], zs.at[12], zr.at[12]
    )
    z_q.start()
    d1[1].early()
    d1[1].last()
    out_sc[1].early()
    out_sc[1].last()
    R.gws[...] = wo_sc.finish().astype(bf16)
    z_o = to_planes_part(
        lambda other: R.gws.at[pl.ds(pl.multiple_of(other * 32, 32), 32)], R.zo, 15
    )

    R.gdo[...] = z_down.finish().astype(bf16)
    for copy in z_b:
        copy.wait_recv()
    bz_all = bz[...] + (R.zb[ring.up(1)] + R.zb[ring.up(2)] + R.zb[ring.up(3)])
    R.bzs[...] = bz_all
    own_up = jnp.zeros((1, head), f32)
    for k in range(4):
        own_up = jnp.where(layer == k, bz_all[2 + k : 3 + k, :], own_up)
    R.bu[...] = jnp.broadcast_to(own_up, (8, head))
    psem = R.ps
    home_copies = (
        (R.gdo, R.o_gd, psem.at[0], psem.at[2], psem.at[3]),
        (R.bu, R.o_bu, psem.at[1], psem.at[4], psem.at[5]),
    )

    @pl.when(at_home)
    def _():
        for src, dst, sem, _, _ in home_copies:
            move(src, dst, sem).wait()

    away = [
        Sent(src, dst, ssem, rsem, (owner_col, owner_layer))
        for src, dst, _, ssem, rsem in home_copies
    ]

    @pl.when(jnp.logical_not(at_home))
    def _():
        for copy in away:
            copy.start()

    def to_columns(src, dst, row):
        keep = move(src.at[col], dst.at[col], local.at[21 + row])
        copies = []
        for slot, other in enumerate(others):
            copies.append(
                send(
                    src.at[other],
                    dst.at[col],
                    R.a_s.at[4 + row, slot],
                    R.a_r.at[4 + row, slot],
                    ring.flat(other),
                )
            )
        return keep, copies

    R.guo[...] = z_up.finish().astype(bf16)
    up_keep, up_moves = to_columns(R.guo, R.o_gu, 0)

    bias_d = params_row(7)
    for s in range(2):
        R.los[s] = (R.r1[s] + out_sc[s].finish() + bias_d).astype(bf16)
    save_lo = move(R.los, R.o_lo, local.at[24])

    def back_norm1(s):
        grad = d1[s].finish()
        normed, inv_dev = row_norm(R.xb[s].astype(f32))
        scaled = grad * gain1
        total = R.dr[s] + inv_dev * (
            scaled
            - jnp.mean(scaled, axis=-1, keepdims=True)
            - normed * jnp.mean(scaled * normed, axis=-1, keepdims=True)
        )
        R.igs[s] = total.astype(bf16)
        for row, item in ((4, grad * normed), (5, grad)):
            item = jnp.sum(item, axis=0, keepdims=True)
            sums[row] = sums[row] + item if row in sums else item

    back_norm1(0)
    z_q.middle()
    back_norm1(1)
    save_ig = move(R.igs, R.o_ig, local.at[23])
    for row in range(6):
        R.ev[row : row + 1, :] = sums[row]
    R.ev[6:8, :] = jnp.zeros((2, width), f32)
    ev_moves = []
    for hop in range(1, 8):
        other = (col + hop) % 8
        ev_moves.append(
            send(
                R.ev.at[:, pl.ds(pl.multiple_of(other * head, head), head)],
                R.evr.at[hop - 1],
                R.es.at[hop - 1],
                R.er.at[hop - 1],
                ring.flat(other),
            )
        )
    R.gqo[...] = z_q.finish().astype(bf16)
    q_keep, q_moves = to_columns(R.gqo, R.o_gq, 1)
    for copy in ev_moves:
        copy.wait_recv()
    plane = R.ev[:, pl.ds(head_cols, head)]
    for k in range(7):
        plane = plane + R.evr[k]
    R.evp[...] = plane
    z_e = to_planes(R.evp, R.evz.at[layer], 14)
    for copy in z_o:
        copy.wait_recv()
    go_rows = pl.ds(pl.multiple_of(layer * 32, 32), 32)
    total = R.gws[go_rows].astype(f32)
    for k in range(3):
        total = total + R.zo[k].astype(f32)
    R.o_go[...] = total
    for copy in z_e:
        copy.wait_recv()
    total = R.evp[...] + (R.evz[ring.up(1)] + R.evz[ring.up(2)] + R.evz[ring.up(3)])
    both = jnp.concatenate([total, R.bzs[...]], axis=0)
    picked = jnp.zeros((16, 32), f32)
    for k in range(4):
        picked = jnp.where(layer == k, both[:, k * 32 : (k + 1) * 32], picked)
    R.o_small[...] = picked

    @pl.when(jnp.logical_not(at_home))
    def _():
        for copy in away:
            copy.wait_recv()
            copy.wait_send()

    save_ig.wait()
    save_lo.wait()
    for keep, copies in ((up_keep, up_moves), (q_keep, q_moves)):
        keep.wait()
        for copy in copies:
            copy.wait_recv()
    wire.drain()
    for chain in (chain_q, chain_u, chain_d):
        chain.drain()


def closing_kernel(refs):
    R = refs
    f32 = jnp.float32
    head = HEAD_DIM
    sem = R.sem
    plan = (
        (R.gd, R.vd, R.td, R.f_gd),
        (R.gu, R.vu, R.tu, R.f_gu),
        (R.gq, R.vq, R.tq, R.f_gq),
        (R.lo, R.vl, R.vl, R.f_lo),
        (R.ig, R.vi, R.vi, R.f_ig),
        (R.go, R.vo, R.vo, R.f_go),
    )
    loads = [move(src, held, sem.at[slot]) for slot, (src, held, _, _) in enumerate(plan)]
    waits = []
    for slot, (_, held, wide, dst) in enumerate(plan):
        loads[slot].wait()
        if slot == 0:
            wide[...] = held[...].astype(f32)
        elif slot < 3:
            groups = held.shape[2] // head
            for g in range(groups):
                for c in range(8):
                    first = (g * 8 + c) * head
                    piece = held[c, :, g * head : (g + 1) * head]
                    wide[:, first : first + head] = piece.astype(f32)
        waits.append(move(wide, dst, sem.at[6 + slot]))
    for row, ref in R.rows:
        ref[...] = R.small[row]
    R.f_bu[...] = R.bu[0]
    for copy in waits:
        copy.wait()

def per_device_tp(
    layer_in,
    block_order,
    ln1_gain,
    ln1_shift,
    w_qkv,
    b_query,
    b_value,
    w_out,
    b_out,
    ln2_gain,
    ln2_shift,
    w_up,
    b_up,
    w_down,
    b_down,
    cotangent,
):
    f32, bf16, i32 = jnp.float32, jnp.bfloat16, jnp.int32
    seqs, tokens, width = layer_in.shape
    seq_len = tokens * 8
    ff = w_up.shape[1]
    hid = ff // 32
    vectors = [
        item.reshape(2, -1)
        for item in (ln1_gain, ln1_shift, b_query, b_value, b_out, ln2_gain, ln2_shift, b_down)
    ]
    anywhere = pl.BlockSpec(memory_space=pl.ANY)
    in_vmem = pl.BlockSpec(memory_space=pltpu.VMEM)
    inputs = dict(
        order=(block_order, pl.BlockSpec(memory_space=pltpu.SMEM)),
        b_up=(b_up.reshape(8, -1), anywhere),
        x=(layer_in, anywhere),
        cot=(cotangent, anywhere),
        w_qkv=(w_qkv, anywhere),
        w_out=(w_out, anywhere),
        w_up=(w_up, anywhere),
        w_down=(w_down, anywhere),
    )
    outputs = dict(
        o_lo=((seqs, tokens, width), bf16, anywhere),
        o_ig=((seqs, tokens, width), bf16, anywhere),
        o_gq=((8, 32, 3 * HEAD_DIM), bf16, anywhere),
        o_gu=((8, 32, 4 * hid), bf16, anywhere),
        o_gd=((hid, width), bf16, anywhere),
        o_go=((32, width), f32, in_vmem),
        o_small=((16, 32), f32, in_vmem),
        o_bu=((8, HEAD_DIM), f32, anywhere),
    )
    whole = (seqs, seq_len, width)
    heads = (seqs, seq_len, HEAD_DIM)
    turned = (seqs, HEAD_DIM, seq_len)
    own = (seqs, tokens, width)
    vmem, sems = pltpu.VMEM, pltpu.SemaphoreType.DMA
    scratch = dict(
        h1=vmem(whole, bf16),
        ct=vmem(whole, bf16),
        h2=vmem(whole, bf16),
        po=vmem(whole, bf16),
        pd=vmem(whole, bf16),
        wq=vmem((width, 3 * HEAD_DIM), bf16),
        wo=vmem((4, 8, 32, width), bf16),
        wu=vmem((width, 4 * hid), bf16),
        wd=vmem((4 * hid, width), bf16),
        q=vmem(heads, bf16),
        k=vmem(heads, bf16),
        v=vmem(heads, bf16),
        kt=vmem(turned, bf16),
        vt=vmem(turned, bf16),
        ol=vmem(heads, bf16),
        dh=vmem(heads, bf16),
        ob=vmem(own, bf16),
        db=vmem(own, bf16),
        xb=vmem(own, bf16),
        dz=vmem(own, bf16),
        igs=vmem(own, bf16),
        los=vmem(own, bf16),
        r1=vmem(own, f32),
        dr=vmem(own, f32),
        r_sib=vmem((5, 4, tokens, width), bf16),
        r_diag=vmem((5, 2, tokens // 2, width), bf16),
        r_side=vmem((5, 2, tokens, width), bf16),
        kpos=vmem(heads, i32),
        qpos=vmem((seqs, 1, seq_len), i32),
        lse=vmem((seqs, 1, seq_len), f32),
        act=vmem((seqs, seq_len, 4 * hid), bf16),
        du=vmem((seqs, seq_len, 4 * hid), bf16),
        dp=vmem((seqs, seq_len, 3 * HEAD_DIM), bf16),
        dka=vmem(heads, f32),
        dva=vmem(heads, f32),
        gd=vmem((4 * hid, width), bf16),
        gu=vmem((8, 4, 32, 4 * hid), bf16),
        gq=vmem((8, 4, 32, 3 * HEAD_DIM), bf16),
        gws=vmem((tokens, width), bf16),
        gdo=vmem((hid, width), bf16),
        guo=vmem((8, 32, 4 * hid), bf16),
        gqo=vmem((8, 32, 3 * HEAD_DIM), bf16),
        zd=vmem((3, hid, width), bf16),
        zu=vmem((3, 8, 32, 4 * hid), bf16),
        zq=vmem((3, 8, 32, 3 * HEAD_DIM), bf16),
        zo=vmem((3, 32, width), bf16),
        pv=vmem((4, 8, 2, HEAD_DIM), bf16),
        pb=vmem((4, 8, HEAD_DIM), bf16),
        us=vmem((1, 4 * hid), f32),
        bz=vmem((8, HEAD_DIM), f32),
        bzs=vmem((8, HEAD_DIM), f32),
        bu=vmem((8, HEAD_DIM), f32),
        zb=vmem((4, 8, HEAD_DIM), f32),
        ev=vmem((8, width), f32),
        evr=vmem((7, 8, HEAD_DIM), f32),
        evp=vmem((8, HEAD_DIM), f32),
        evz=vmem((4, 8, HEAD_DIM), f32),
        lsem=sems((25,)),
        zs=sems((16, 3)),
        zr=sems((16, 3)),
        cs=sems((3, 2, 3)),
        cr=sems((3, 2, 3)),
        gs=sems((7, 10)),
        gr=sems((7, 10)),
        ss=sems((7, 10)),
        sr=sems((7, 10)),
        a_s=sems((6, 7)),
        a_r=sems((6, 7)),
        es=sems((7,)),
        er=sems((7,)),
        ps=sems((6,)),
    )
    names = list(inputs) + list(outputs) + list(scratch)

    def body(*refs):
        space = types.SimpleNamespace(**dict(zip(names, refs[8:])))
        space.vectors = refs[:8]
        layer_kernel(HEAD_DIM ** (-0.5), space)

    results = pl.pallas_call(
        body,
        out_shape=[jax.ShapeDtypeStruct(shape, kind) for shape, kind, _ in outputs.values()],
        in_specs=[anywhere] * 8 + [spec for _, spec in inputs.values()],
        out_specs=[spec for _, _, spec in outputs.values()],
        scratch_shapes=list(scratch.values()),
        compiler_params=pltpu.CompilerParams(
            collective_id=0, has_side_effects=True, vmem_limit_bytes=VMEM_BYTES
        ),
    )(*vectors, *(item for item, _ in inputs.values()))
    finals = dict(
        f_lo=((seqs, tokens, width), bf16, anywhere),
        f_ig=((seqs, tokens, width), bf16, anywhere),
        f_g1=((32,), f32, in_vmem),
        f_s1=((32,), f32, in_vmem),
        f_gq=((32, 3 * width), f32, anywhere),
        f_bq=((32,), f32, in_vmem),
        f_bv=((32,), f32, in_vmem),
        f_go=((32, width), f32, anywhere),
        f_bo=((32,), f32, in_vmem),
        f_g2=((32,), f32, in_vmem),
        f_s2=((32,), f32, in_vmem),
        f_gu=((32, ff), f32, anywhere),
        f_bu=((HEAD_DIM,), f32, in_vmem),
        f_gd=((hid, width), f32, anywhere),
        f_bd=((32,), f32, in_vmem),
    )
    held = dict(
        vd=vmem((hid, width), bf16),
        vu=vmem((8, 32, 4 * hid), bf16),
        vq=vmem((8, 32, 3 * HEAD_DIM), bf16),
        td=vmem((hid, width), f32),
        tu=vmem((32, ff), f32),
        tq=vmem((32, 3 * width), f32),
        vl=vmem(own, bf16),
        vi=vmem(own, bf16),
        vo=vmem((32, width), f32),
        sem=sems((12,)),
    )
    last_names = [item[2:] for item in outputs] + list(finals) + list(held)

    def last_body(*refs):
        space = types.SimpleNamespace(**dict(zip(last_names, refs)))
        space.rows = (
            (4, space.f_g1),
            (5, space.f_s1),
            (8, space.f_bq),
            (9, space.f_bv),
            (0, space.f_bo),
            (1, space.f_g2),
            (2, space.f_s2),
            (3, space.f_bd),
        )
        closing_kernel(space)

    return tuple(
        pl.pallas_call(
            last_body,
            out_shape=[jax.ShapeDtypeStruct(shape, kind) for shape, kind, _ in finals.values()],
            in_specs=[anywhere] * 6 + [in_vmem] * 2,
            out_specs=[spec for _, _, spec in finals.values()],
            scratch_shapes=list(held.values()),
        )(*results)
    )


def solution(mesh):
    placed = (
        P("fsdp", "ctx", None),
        P("fsdp", None),
        P("fsdp"),
        P("fsdp"),
        P("fsdp", None),
        P("fsdp"),
        P("fsdp"),
        P("fsdp", None),
        P("fsdp"),
        P("fsdp"),
        P("fsdp"),
        P("fsdp", None),
        P("fsdp"),
        P("fsdp", None),
        P("fsdp"),
        P("fsdp", "ctx", None),
    )
    by_heads = mesh.shape["ctx"] == HEADS and mesh.shape["fsdp"] == 4
    return jax.shard_map(
        per_device_tp if by_heads else per_device_ctx,
        mesh=mesh,
        in_specs=placed,
        out_specs=(
            P("fsdp", "ctx", None),
            P("fsdp", "ctx", None),
            P(("ctx", "fsdp")),
            P(("ctx", "fsdp")),
            P(("ctx", "fsdp"), None),
            P(("ctx", "fsdp")),
            P(("ctx", "fsdp")),
            P(("ctx", "fsdp"), None),
            P(("ctx", "fsdp")),
            P(("ctx", "fsdp")),
            P(("ctx", "fsdp")),
            P(("ctx", "fsdp"), None),
            P(("ctx", "fsdp")),
            P(("ctx", "fsdp"), None),
            P(("ctx", "fsdp")),
        ),
        check_vma=False,
    )
```

profile of v0, /device:TPU:0, one launch (start us, length us, event | category | flops | bytes accessed | tf_op | source)
XLA Modules:
  0.0 171.4 jit_solution(9439933315243530313)
XLA Ops:
  0.7 166.8 %shard_map.271 = (bf16[2,128,1024]{2,1,0:T(8,128)(2,1)}, bf16[2,128,1024]{2,1,0:T(8,128)(2,1)}, bf16[8,32,384]{2,1,0:T(8,128)(2,1)}, bf16[8,32,512]{2,1,0:T(8,12...) custom-call(bf16[2,128]{1,0:T(2,128)(2,1)} %bitcast.10, ...), custom_call_target="tpu_custom_call" | custom-call | tf_op jit(solution)/shard_map/pallas_call | solution.py:1430
  167.4 3.8 %shard_map.272 = (bf16[2,128,1024]{2,1,0:T(8,128)(2,1)}, bf16[2,128,1024]{2,1,0:T(8,128)(2,1)}, f32[32]{0:T(128)}, f32[32]{0:T(128)}, f32[32,3072]{1,0:T(8,128)}...) custom-call(bf16[2,128,1024]{2,1,0:T(8,128)(2,1)} %get-tuple-element, ...), custom_call_target="tpu_custom_call" | custom-call | tf_op jit(solution)/shard_map/pallas_call | solution.py:1486
where the time goes:
time: 172 us; the launch traced here: 171 us
  Pallas kernels  171 us (99%)
    pallas_call x1, Pallas kernels, per_device_tp(): pl.pallas_call(body, out_shape=[jax.ShapeDtypeStruct(shape, kind) for sha...  167 us
    pallas_call x1, Pallas kernels, per_device_tp(): pl.pallas_call(last_body, out_shape=[jax.ShapeDtypeStruct(shape, kind) fo...  3.82 us

commit v1 on v0

--- a/solution.py
+++ b/solution.py
@@ -659,11 +659,15 @@
     me = col * 4 + layer
     owner_col, owner_layer = 2 * layer + col // 4, col % 4
     at_home = owner_col * 4 + owner_layer == me
-    for hop in range(1, 32):
-        other = (me + hop) % 32
-        pl.semaphore_signal(
-            barrier, 1, device_id=(other // 4, other % 4), device_id_type=pl.DeviceIdType.MESH
-        )
+    giver = (col % 2 * 4 + layer) * 4 + col // 2
+    moved = ((owner_col * 4 + owner_layer - me + 32) % 32 + 31) // 32
+    peers = [((col + hop) % 8, layer) for hop in range(1, 8)]
+    peers += [(col, ring.up(hop)) for hop in range(1, 4)]
+    for other in (owner_col * 4 + owner_layer, giver):
+        other = moved * other + (1 - moved) * (31 - me)
+        peers.append((other // 4, other % 4))
+    for where in peers:
+        pl.semaphore_signal(barrier, 1, device_id=where, device_id_type=pl.DeviceIdType.MESH)
     local = R.lsem
     load_x = move(R.x, R.xb, local.at[0])
     load_ct = [move(R.cot.at[s], R.ct.at[s, mine], local.at[1 + s]) for s in range(seqs)]
@@ -703,7 +707,7 @@
     for copy in load_p:
         copy.wait()
     load_b.wait()
-    pl.semaphore_wait(barrier, 31)
+    pl.semaphore_wait(barrier, 12)
 
     zs, zr = R.zs, R.zr
 
@@ -805,6 +809,14 @@
         place_x = chip_x + flip_x - 2 * chip_x * flip_x
         place_y = chip_y + flip_y - 2 * chip_y * flip_y
         return place_x + 2 * place_y, flip_x + 2 * flip_y
+
+    def pairs(body, **between):
+        @pl.loop(0, 2)
+        def _(high):
+            body((high, 0))
+            body((high, 1))
+            for name, action in between.items():
+                pl.when(high == int(name[1:]))(action)
 
     def tiles(body, **between):
         @pl.loop(0, 2)
@@ -904,7 +916,7 @@
     for copy in send_o:
         copy.wait_recv()
     wo_gather.start()
-    tiles(lambda t: attend(0, t), t2=wo_gather.relay)
+    pairs(lambda t: attend(0, t), t0=wo_gather.relay)
     moved_o = [heads_to_rows(0)]
     h1_gather[1].finish()
     ct_gather[1].relay()
@@ -937,6 +949,7 @@
         chip, slot = order(t)
         r = span(chip)
         hidden = dot_nn(R.h2[s, r, :], R.wu[...]) + bias_u
+        grad = dot_nt(R.ct[s, r, :], R.wd[...])
         square = hidden * hidden
         bend = jnp.tanh(hidden * (GELU_C + (GELU_C * GELU_K) * square))
         half = 0.5 * (1.0 + bend)
@@ -945,11 +958,10 @@
             GELU_C + (3.0 * GELU_C * GELU_K) * square
         )
         R.act[s, r, :] = active
-        R.po[s, r, :] = dot_nn(active, R.wd[...]).astype(bf16)
-        grad = dot_nt(R.ct[s, r, :], R.wd[...])
         grad = (grad * slope).astype(bf16)
         R.du[s, r, :] = grad
         R.pd[s, r, :] = dot_nt(grad, R.wu[...]).astype(bf16)
+        R.po[s, r, :] = dot_nn(active, R.wd[...]).astype(bf16)
         R.us[...] += jnp.sum(grad.astype(f32), axis=0, keepdims=True)
         d2[s].start_of(chip, slot)
         out_sc[s].start_of(chip, slot)
@@ -970,17 +982,15 @@
     R.us[...] = jnp.zeros_like(R.us)
     d2 = [scatter(R.pd.at[s], s, s, s) for s in range(2)]
     out_sc = [scatter(R.po.at[s], s, 2 + s, 2 + s) for s in range(2)]
-    tiles(
+    pairs(
         lambda t: feed(0, t),
-        t0=h2_gather[1].relay,
-        t1=d2[0].middle,
-        t2=h2_gather[1].relay_diag,
-        t3=d2[0].early,
+        t0=many(h2_gather[1].relay, d2[0].middle),
+        t1=many(h2_gather[1].relay_diag, d2[0].early),
     )
     d2[0].last()
     h2_gather[1].finish()
     ct_gather[1].finish()
-    tiles(lambda t: feed(1, t), t1=d2[1].middle, t3=d2[1].early)
+    pairs(lambda t: feed(1, t), t0=d2[1].middle, t1=d2[1].early)
 
     bz = R.bz
     for g in range(4):
@@ -1091,7 +1101,7 @@
     R.dka[...] = jnp.zeros_like(R.dka)
     for copy in moved_d[0]:
         copy.wait_recv()
-    tiles(lambda t: attend_back(0, t), t1=wo_sc.middle)
+    pairs(lambda t: attend_back(0, t), t0=wo_sc.middle)
     close_back(0)
     d2[0].drain()
     d1 = [scatter(R.pd.at[s], s, s, 4 + s) for s in range(2)]

time: 172 us -> 169 us (0.983)
  Pallas kernels: 171 us -> 168 us
    pallas_call x1, Pallas kernels: 167 us -> 164 us  [per_device_tp(): pl.pallas_call(body, out_shape=[jax.ShapeDtypeStruct(shape, kind) for sha...]
where the time goes in v1:
time: 169 us
  Pallas kernels  168 us (99%)
    pallas_call x1, Pallas kernels, per_device_tp(): pl.pallas_call(body, out_shape=[jax.ShapeDtypeStruct(shape, kind) for sha...  164 us
    pallas_call x1, Pallas kernels, per_device_tp(): pl.pallas_call(last_body, out_shape=[jax.ShapeDtypeStruct(shape, kind) fo...  3.82 us

profile of v1, /device:TPU:0, one launch (start us, length us, event | category | flops | bytes accessed | tf_op | source)
XLA Modules:
  0.0 169.1 jit_solution(5324935887327250976)
XLA Ops:
  0.7 164.5 %shard_map.271 = (bf16[2,128,1024]{2,1,0:T(8,128)(2,1)}, bf16[2,128,1024]{2,1,0:T(8,128)(2,1)}, bf16[8,32,384]{2,1,0:T(8,128)(2,1)}, bf16[8,32,512]{2,1,0:T(8,12...) custom-call(bf16[2,128]{1,0:T(2,128)(2,1)} %bitcast.10, ...), custom_call_target="tpu_custom_call" | custom-call | tf_op jit(solution)/shard_map/pallas_call | solution.py:1440
  165.1 3.8 %shard_map.272 = (bf16[2,128,1024]{2,1,0:T(8,128)(2,1)}, bf16[2,128,1024]{2,1,0:T(8,128)(2,1)}, f32[32]{0:T(128)}, f32[32]{0:T(128)}, f32[32,3072]{1,0:T(8,128)}...) custom-call(bf16[2,128,1024]{2,1,0:T(8,128)(2,1)} %get-tuple-element, ...), custom_call_target="tpu_custom_call" | custom-call | tf_op jit(solution)/shard_map/pallas_call | solution.py:1496

commit v2 on v1

--- a/solution.py
+++ b/solution.py
@@ -928,11 +928,10 @@
         out_project(0)
         h2_gather[0].start()
 
-    tiles(
+    pairs(
         lambda t: attend(1, t),
-        t0=lambda: chain_d.pass_on(1),
-        t1=many(wo_gather.finish, first_rows),
-        t2=ct_gather[1].relay_diag,
+        t0=many(lambda: chain_d.pass_on(1), wo_gather.finish, first_rows),
+        t1=ct_gather[1].relay_diag,
     )
     moved_o.append(heads_to_rows(1))
     h2_gather[0].relay()

time: 169 us -> 170 us (level)
  no operation moved by 1% of the time
where the time goes in v2:
time: 170 us; the launch traced here: 169 us
  Pallas kernels  168 us (99%)
    pallas_call x1, Pallas kernels, per_device_tp(): pl.pallas_call(body, out_shape=[jax.ShapeDtypeStruct(shape, kind) for sha...  165 us
    pallas_call x1, Pallas kernels, per_device_tp(): pl.pallas_call(last_body, out_shape=[jax.ShapeDtypeStruct(shape, kind) fo...  3.82 us

profile of v2, /device:TPU:0, one launch (start us, length us, event | category | flops | bytes accessed | tf_op | source)
XLA Modules:
  0.0 169.2 jit_solution(739250230131868879)
XLA Ops:
  0.7 164.6 %shard_map.271 = (bf16[2,128,1024]{2,1,0:T(8,128)(2,1)}, bf16[2,128,1024]{2,1,0:T(8,128)(2,1)}, bf16[8,32,384]{2,1,0:T(8,128)(2,1)}, bf16[8,32,512]{2,1,0:T(8,12...) custom-call(bf16[2,128]{1,0:T(2,128)(2,1)} %bitcast.10, ...), custom_call_target="tpu_custom_call" | custom-call | tf_op jit(solution)/shard_map/pallas_call | solution.py:1439
  165.2 3.8 %shard_map.272 = (bf16[2,128,1024]{2,1,0:T(8,128)(2,1)}, bf16[2,128,1024]{2,1,0:T(8,128)(2,1)}, f32[32]{0:T(128)}, f32[32]{0:T(128)}, f32[32,3072]{1,0:T(8,128)}...) custom-call(bf16[2,128,1024]{2,1,0:T(8,128)(2,1)} %get-tuple-element, ...), custom_call_target="tpu_custom_call" | custom-call | tf_op jit(solution)/shard_map/pallas_call | solution.py:1495
